TPU v7x, 128 devices: a whole 4x4x4 slice. The times are simulated.
128 devices in a mesh: pts: 32 (over x, y, core), grp: 4 (over z).
Axes of the slice: x: 4, y: 4, z: 4, core: 2. Of those that a mesh axis runs over, the one named last changes fastest.
Arguments:
- points: bfloat16 [262144, 256], P(('pts', 'grp')), may hold values from -6 to 6
- cotangent: bfloat16 [262144, 256], P(('pts', 'grp')), may hold values from -24 to 24
- gain_one: float32 [256], replicated, may hold values from 0.25 to 1.75
- gain_two: float32 [256], replicated, may hold values from 0.25 to 1.75
- w_mid: bfloat16 [256, 256], replicated, may hold values from -0.375 to 0.375
- w_feat: bfloat16 [256, 256], replicated, may hold values from -0.375 to 0.375
- w_out: bfloat16 [256, 256], replicated, may hold values from -0.375 to 0.375
- w_up: bfloat16 [256, 1024], replicated, may hold values from -0.375 to 0.375
- w_down: bfloat16 [256, 1024], replicated, may hold values from -0.1875 to 0.1875
- w_slice: float32 [32, 32], replicated, as said below
- w_temp: float32 [32], replicated, may hold values from -2 to 2
- query_matrix: float32 [32, 32], replicated
- key_matrix: float32 [32, 32], replicated
- value_matrix: float32 [32, 32], replicated, may hold values from -1 to 1
Outputs:
- grad_points: bfloat16 [262144, 256], P(('pts', 'grp'))
- grad_mid: float32 [256, 256], replicated
- grad_feat: float32 [256, 256], replicated
- grad_out: float32 [256, 256], replicated
- grad_up: float32 [256, 1024], replicated
- grad_down: float32 [256, 1024], replicated
- grad_gain_one: float32 [256], replicated
- grad_gain_two: float32 [256], replicated
- grad_slice: float32 [32, 32], replicated
- grad_temp: float32 [32], replicated
- grad_query: float32 [32, 32], replicated
- grad_key: float32 [32, 32], replicated
- grad_value: float32 [32, 32], replicated
Inputs may be any that keep to these rules, and one draw needn't show every extreme that they name: w_slice is a real matrix.
All inputs are finite; a program needn't handle non-finite values.
Results may differ from a plain program's by a relative error of at most 0.023.
The roundings to bfloat16 on the way count: a program that leaves them out, or rounds other values in their place, can miss the bound.
Values sent between devices are 32-bit elements; how exact they have to be, the bound alone decides.
A program may use at most 128 MiB of HBM per device.

v0:
```python
import jax
import jax.numpy as jnp
from jax import lax
from jax.sharding import PartitionSpec as P

HEADS = 8
HEAD_DIM = 32


EPS_NORM = 1e-05
EPS_SLICE = 1e-05
PRECISION_LEVEL = lax.Precision.HIGHEST


def layer_norm(value_rows, gain):
    centred = value_rows - jnp.mean(value_rows, axis=-1, keepdims=True)
    spread_tokens = jnp.mean(centred * centred, axis=-1, keepdims=True)
    return centred * lax.rsqrt(spread_tokens + EPS_NORM) * gain


def assign(middle, w_slice, w_temp):
    temper = 0.5 + jax.nn.softplus(
        jnp.einsum("nhd,d->nh", middle, w_temp, precision=PRECISION_LEVEL)
    )
    logits = (
        jnp.einsum("nhd,dm->nhm", middle, w_slice, precision=PRECISION_LEVEL) / temper[:, :, None]
    )
    return jax.nn.softmax(logits, axis=-1)


def mix_tokens(numerator_sums, denom, query_matrix, key_matrix, value_matrix):
    slice_token_rows = numerator_sums / (denom[:, :, None] + EPS_SLICE)
    query_rows = jnp.einsum(
        "xsf,fz->xsz", slice_token_rows, query_matrix, precision=PRECISION_LEVEL
    )
    key_rows = jnp.einsum("xsf,fz->xsz", slice_token_rows, key_matrix, precision=PRECISION_LEVEL)
    value_rows = jnp.einsum(
        "xsf,fz->xsz", slice_token_rows, value_matrix, precision=PRECISION_LEVEL
    )
    scores = jnp.einsum(
        "hme,hne->hmn", query_rows, key_rows, precision=PRECISION_LEVEL
    ) * slice_token_rows.shape[-1] ** (-0.5)
    probs = jax.nn.softmax(scores, axis=-1)
    return jnp.einsum("hmn,hne->hme", probs, value_rows, precision=PRECISION_LEVEL)


def transposed(left, right):
    return lax.dot_general(
        left, right, (((0,), (0,)), ((), ())), preferred_element_type=jnp.float32
    )


def against(left, right):
    return lax.dot_general(
        left, right, (((1,), (1,)), ((), ())), preferred_element_type=jnp.float32
    )


def local(
    points,
    cotangent,
    gain_one,
    gain_two,
    w_mid,
    w_feat,
    w_out,
    w_up,
    w_down,
    w_slice,
    w_temp,
    query_matrix,
    key_matrix,
    value_matrix,
):
    rows = points.shape[0]
    width = w_mid.shape[0]
    hidden_units = w_up.shape[1]
    points_f = points.astype(jnp.float32)
    normed = layer_norm(points_f, gain_one).astype(jnp.bfloat16)
    middle = jnp.dot(normed, w_mid, preferred_element_type=jnp.float32).astype(jnp.bfloat16)
    feats = jnp.dot(normed, w_feat, preferred_element_type=jnp.float32).astype(jnp.bfloat16)
    middle_f = middle.astype(jnp.float32).reshape(rows, HEADS, HEAD_DIM)
    weights = assign(middle_f, w_slice, w_temp)
    weight_rows_low = weights.astype(jnp.bfloat16)
    feature_rows_three = feats.reshape(rows, HEADS, HEAD_DIM)
    numerator_sums = jnp.einsum(
        "gux,guj->uxj", weight_rows_low, feature_rows_three, preferred_element_type=jnp.float32
    )
    denom = jnp.sum(weights, axis=0)
    numerator_sums, denom = lax.psum((numerator_sums, denom), ("pts", "grp"))
    mixed_token_low = mix_tokens(
        numerator_sums, denom, query_matrix, key_matrix, value_matrix
    ).astype(jnp.bfloat16)
    spread_tokens = jnp.einsum(
        "lge,gex->lgx", weight_rows_low, mixed_token_low, preferred_element_type=jnp.float32
    )
    spread_tokens = spread_tokens.astype(jnp.bfloat16).reshape(rows, width)
    resid = (points_f + jnp.dot(spread_tokens, w_out, preferred_element_type=jnp.float32)).astype(
        jnp.bfloat16
    )
    resid_f = resid.astype(jnp.float32)
    normed_two = layer_norm(resid_f, gain_two).astype(jnp.bfloat16)
    pre = jnp.dot(normed_two, w_up, preferred_element_type=jnp.float32)
    hidden = jax.nn.gelu(pre).astype(jnp.bfloat16)
    d_hid = jnp.dot(cotangent, w_down, preferred_element_type=jnp.float32)
    gelu_back = jax.vjp(jax.nn.gelu, pre)[1]
    d_pre = gelu_back(d_hid)[0].astype(jnp.bfloat16)
    d_norm_two = against(d_pre, w_up)
    norm_back_two = jax.vjp(layer_norm, resid_f, gain_two)[1]
    d_res_ln, d_gain_two = norm_back_two(d_norm_two)
    d_resid = cotangent.astype(jnp.float32) + d_res_ln
    d_resid_b = d_resid.astype(jnp.bfloat16)
    spread_gradient = against(d_resid_b, w_out).astype(jnp.bfloat16).reshape(rows, HEADS, HEAD_DIM)
    mixed_gradient = jnp.einsum(
        "gux,guj->uxj", weight_rows_low, spread_gradient, preferred_element_type=jnp.float32
    )
    mixed_gradient = lax.psum(mixed_gradient, ("pts", "grp"))
    token_back = jax.vjp(mix_tokens, numerator_sums, denom, query_matrix, key_matrix, value_matrix)[
        1
    ]
    numerator_gradient, denominator_gradient, grad_query, grad_key, grad_value = token_back(
        mixed_gradient
    )
    weight_gradient = jnp.einsum(
        "wkt,klt->wkl", spread_gradient, mixed_token_low, preferred_element_type=jnp.float32
    )
    weight_gradient = (
        weight_gradient
        + jnp.einsum("wkt,klt->wkl", feature_rows_three.astype(jnp.float32), numerator_gradient)
        + denominator_gradient[None, :, :]
    )
    feature_gradient = jnp.einsum(
        "lge,gex->lgx", weight_rows_low.astype(jnp.float32), numerator_gradient
    )
    feature_gradient = feature_gradient.astype(jnp.bfloat16).reshape(rows, width)
    assign_back = jax.vjp(assign, middle_f, w_slice, w_temp)[1]
    d_mid, d_slice, d_temp = assign_back(weight_gradient)
    d_mid = d_mid.reshape(rows, width).astype(jnp.bfloat16)
    d_normed = against(d_mid, w_mid) + against(feature_gradient, w_feat)
    norm_back_one = jax.vjp(layer_norm, points_f, gain_one)[1]
    d_ln, d_gain_one = norm_back_one(d_normed)
    grad_points = (d_resid + d_ln).astype(jnp.bfloat16)

    def rows_of(left, right):
        return transposed(left, right)

    big = lax.psum(
        jnp.concatenate(
            [
                rows_of(normed, d_mid),
                rows_of(normed, feature_gradient),
                rows_of(spread_tokens, d_resid_b),
                rows_of(normed_two, d_pre),
                rows_of(cotangent, hidden),
            ],
            axis=1,
        ),
        ("pts", "grp"),
    )
    g_slice, g_temp, g_one, g_two = lax.psum(
        (d_slice, d_temp, d_gain_one, d_gain_two), ("pts", "grp")
    )
    return (
        grad_points,
        big[:, :width],
        big[:, width : 2 * width],
        big[:, 2 * width : 3 * width],
        big[:, 3 * width : 3 * width + hidden_units],
        big[:, 3 * width + hidden_units :],
        g_one,
        g_two,
        g_slice,
        g_temp,
        grad_query,
        grad_key,
        grad_value,
    )


def solution(mesh):
    return jax.shard_map(
        local,
        mesh=mesh,
        in_specs=(
            P(("pts", "grp"), None),
            P(("pts", "grp"), None),
            P(),
            P(),
            P(),
            P(),
            P(),
            P(),
            P(),
            P(),
            P(),
            P(),
            P(),
            P(),
        ),
        out_specs=(
            P(("pts", "grp"), None),
            P(),
            P(),
            P(),
            P(),
            P(),
            P(),
            P(),
            P(),
            P(),
            P(),
            P(),
            P(),
        ),
        check_vma=False,
    )
```

profile of v0, /device:TPU:1, one launch (start us, length us, event | category | flops | bytes accessed | tf_op | source)
XLA Modules:
  0.0 370.1 jit_solution(17323691424581522889)
XLA Ops:
  7.3 1.6 copy.28
  9.4 1.4 copy.27
  10.8 1.5 convolution_convert_fusion.3
  13.1 2.5 fusion.70
  15.5 6.6 %fusion.74 = f32[1,2048,8]{0,1,2:T(8,128)} fusion(bf16[2048,8,32]{0,2,1:T(8,128)(2,1)S(1)} %bitcast.132, f32[32]{0:T(128)S(1)} %copy-done.57), kind=kOutput, calls=%fused_computation.133 | convolution fusion | flops 6291456 | bytes 1114240 | tf_op jit(solution)/shard_map/nhd,d->nh/dot_general | solution.py:23
  22.1 5.2 %copy.46 = f32[1,2048,8]{1,2,0:T(8,128)S(1)} copy(f32[1,2048,8]{0,1,2:T(8,128)} %fusion.74) | data formatting | bytes 131072 | tf_op jit(solution)/shard_map/nhd,d->nh/dot_general | solution.py:23
  27.4 2.3 fusion.89
  30.1 1.6 copy-done.20
  32.2 70.0 %all-reduce.1 = (f32[8,32,32]{2,1,0:T(8,128)S(1)}, f32[8,32]{1,0:T(8,128)S(1)}) all-reduce(f32[8,32,32]{2,1,0:T(8,128)S(1)} %fusion.91, f32[8,32]{1,0:T(8,128)S(1)} %get-tuple-element.43), channel_id=1, replica_groups=mesh['pts'=32,'grp'=4] {'pts','grp'}, use_global_device_ids=true, to_apply=%region_4.5 | all-reduce | flops 8448 | bytes 67584 | tf_op jit(solution)/shard_map/psum | solution.py:90
  103.2 1.3 fusion.67
  106.8 1.4 fusion.43
  108.3 6.3 %fusion.7 = bf16[2048,1024]{1,0:T(8,128)(2,1)S(1)} fusion(f32[2048,1024]{1,0:T(8,128)S(1)} %fusion.43, bf16[2048,256]{1,0:T(8,128)(2,1)S(1)} %copy-done.27, bf16[256,1024]{1,0:T(8,128)(2,1)S(1)} %copy-done.59), kind=kOutput, calls=%fused_computation.9 | convolution fusion | flops 1115684864 | bytes 14155776 | tf_op jit(solution)/shard_map/dot_general | solution.py:105
  114.6 1.4 fusion.32
  116.5 2.0 fusion.30
  121.8 63.1 %psum.58 = f32[8,32,32]{2,1,0:T(8,128)S(1)} all-reduce(f32[8,32,32]{2,1,0:T(8,128)S(1)} %fusion.93), channel_id=1, replica_groups=mesh['pts'=32,'grp'=4] {'pts','grp'}, use_global_device_ids=true, to_apply=%region_13.14 | all-reduce | flops 8192 | bytes 65536 | tf_op jit(solution)/shard_map/psum | solution.py:117
  185.2 1.3 multiply_reduce_fusion.3
  186.6 1.3 fusion.80
  187.9 1.3 fusion.81
  194.8 2.1 fusion.22
  196.9 1.4 convolution_dynamic-update-slice_fusion.3
  198.3 1.3 convolution_dynamic-update-slice_fusion.2
  201.4 2.3 convolution_dynamic-update-slice_fusion
  203.8 4.3 %fusion.36 = f32[256,2816]{1,0:T(8,128)} fusion(f32[256,2816]{1,0:T(8,128)} %convolution_dynamic-update-slice_fusion, bf16[2048,256]{1,0:T(8,128)(2,1)S(1)} %copy-done.28, f32[2048,1024]{1,0:T(8,128)S(1)} %bitcast.126), kind=kOutput, calls=%fused_computation.60 | convolution fusion | flops 1092616192 | bytes 10485760 | tf_op jit(solution)/shard_map/dot_general | solution.py:48
  208.1 1.8 fusion.94
  210.7 1.5 fusion.28
  212.5 2.5 add_convert_fusion
  215.0 2.3 copy.44
  218.3 2.9 convolution_bitcast_fusion.3
  221.3 64.4 %all-reduce = (f32[256]{0:T(256)}, f32[256]{0:T(256)}, f32[32,32]{1,0:T(8,128)}, f32[32]{0:T(128)}) all-reduce(f32[256]{0:T(256)S(1)} %get-tuple-element.28, f32[256]{0:T(256)S(1)} %copy-done.56, f32[32,32]{1,0:T(8,128)S(1)} %convolution_bitcast_fusion.3, ...), channel_id=1, replica_groups=mesh['pts'=32,'grp'=4] {'pts','grp'}, use_global_device_ids=true, to_apply=%region_22.23 | all-reduce | flops 1568 | bytes 12544 | tf_op jit(solution)/shard_map/psum | solution.py:160
  288.9 69.1 %all-reduce.4.cloned.1.call-done = f32[256,2816]{1,0:T(8,128)} async-done(((f32[256,2816]{1,0:T(8,128)}), f32[256,2816]{1,0:T(8,128)}) %all-reduce.4.cloned.1.call-update) | async-done | bytes 2883600 | tf_op jit(solution)/shard_map/psum | solution.py:147
  358.0 2.0 fusion.88
  360.0 3.1 fusion.87
  (176 shorter events, 21.9 us)
Async XLA Ops:
  7.2 99.6 %copy-start = (bf16[256,1024]{1,0:T(8,128)(2,1)S(1)}, bf16[256,1024]{1,0:T(8,128)(2,1)}, u32[]{:S(2)}) copy-start(bf16[256,1024]{1,0:T(8,128)(2,1)} %param.21) | copy-start | bytes 1572868
  7.2 350.8 %all-reduce.4.cloned.1.call-start = ((), (), s32[]{:S(2)}) async-start(), calls=%async_computation | async-start | bytes 5767168 | tf_op jit(solution)/shard_map/psum | solution.py:147
  9.4 3.0 copy-start.30
  12.9 9.2 %copy-start.18 = (bf16[2048,256]{0,1:T(8,128)(2,1)}, bf16[2048,256]{0,1:T(8,128)(2,1)S(1)}, u32[]{:S(2)}) copy-start(bf16[2048,256]{0,1:T(8,128)(2,1)S(1)} %convolution_convert_fusion.4) | copy-start | bytes 3145732
  12.9 2.6 copy-start.57
  27.4 2.3 copy-start.43
  29.7 2.5 copy-start.6
  29.7 72.5 %copy-start.50 = (f32[32,32]{1,0:T(8,128)S(1)}, f32[32,32]{1,0:T(8,128)}, u32[]{:S(2)}) copy-start(f32[32,32]{1,0:T(8,128)} %param.26) | copy-start | bytes 12292
  30.1 75.2 %copy-start.1 = (bf16[2048,8,32]{0,2,1:T(8,128)(2,1)}, bf16[2048,8,32]{0,2,1:T(8,128)(2,1)S(1)}, u32[]{:S(2)}) copy-start(bf16[2048,8,32]{0,2,1:T(8,128)(2,1)S(1)} %get-tuple-element.44) | copy-start | bytes 3145732
  30.1 72.8 %copy-start.48 = (f32[32,32]{1,0:T(8,128)S(1)}, f32[32,32]{1,0:T(8,128)}, u32[]{:S(2)}) copy-start(f32[32,32]{1,0:T(8,128)} %param.27) | copy-start | bytes 12292
  30.1 73.1 %copy-start.52 = (f32[32,32]{1,0:T(8,128)S(1)}, f32[32,32]{1,0:T(8,128)}, u32[]{:S(2)}) copy-start(f32[32,32]{1,0:T(8,128)} %param.25) | copy-start | bytes 12292
  102.9 3.5 copy-start.33
  102.9 3.0 copy-start.29
  103.2 3.2 copy-start.42
  108.3 6.3 %copy-start.8 = (f32[2048,1024]{1,0:T(8,128)}, f32[2048,1024]{1,0:T(8,128)S(1)}, u32[]{:S(2)}) copy-start(f32[2048,1024]{1,0:T(8,128)S(1)} %fusion.43) | copy-start | bytes 25165828
  116.5 2.9 copy-start.4
  184.9 4.2 %copy-start.12 = (bf16[2048,256]{0,1:T(8,128)(2,1)S(1)}, bf16[2048,256]{0,1:T(8,128)(2,1)}, u32[]{:S(2)}) copy-start(bf16[2048,256]{0,1:T(8,128)(2,1)} %copy-done.11) | copy-start | bytes 3145732
  185.2 4.4 %copy-start.35 = (f32[8,32,32]{2,1,0:T(8,128)}, f32[8,32,32]{2,1,0:T(8,128)S(1)}, u32[]{:S(2)}) copy-start(f32[8,32,32]{2,1,0:T(8,128)S(1)} %fusion.56) | copy-start | bytes 98308
  186.5 3.1 copy-start.49
  187.9 2.3 copy-start.40
  191.6 6.7 %copy-start.22 = (bf16[8,32,2048]{2,1,0:T(8,128)(2,1)}, bf16[8,32,2048]{2,1,0:T(8,128)(2,1)S(1)}, u32[]{:S(2)}) copy-start(bf16[8,32,2048]{2,1,0:T(8,128)(2,1)S(1)} %convolution_convert_fusion.1) | copy-start | bytes 3145732
  194.6 2.2 copy-start.24
  194.7 6.7 %copy-start.61 = (bf16[2048,1024]{1,0:T(8,128)(2,1)S(1)}, bf16[2048,1024]{1,0:T(8,128)(2,1)}, u32[]{:S(2)}) copy-start(bf16[2048,1024]{1,0:T(8,128)(2,1)} %copy-done.60) | copy-start | bytes 12582916
  196.9 2.8 copy-start.25
  196.9 6.9 %slice-start = ((s8[8388608]{0:T(1024)(128)(4,1)}), s8[4194304]{0:T(1024)(128)(4,1)S(1)}, s32[]{:S(2)}) async-start(s8[8388608]{0:T(1024)(128)(4,1)} %bitcast.125), calls=%async_computation.1 | async-start | bytes 8388608
  200.2 3.6 slice-start.1
  201.4 2.3 copy-start.28
  215.0 2.4 copy-start.19
  218.3 2.9 copy-start.56
  218.3 67.3 %copy-start.39 = (f32[8,32,32]{2,1,0:T(8,128)S(1)}, f32[8,32,32]{2,1,0:T(8,128)}, u32[]{:S(2)}) copy-start(f32[8,32,32]{2,1,0:T(8,128)} %copy-done.37) | copy-start | bytes 98308
  218.3 68.4 %copy-start.41 = (f32[8,32,32]{2,1,0:T(8,128)S(1)}, f32[8,32,32]{2,1,0:T(8,128)}, u32[]{:S(2)}) copy-start(f32[8,32,32]{2,1,0:T(8,128)} %copy-done.40) | copy-start | bytes 98308
  218.3 69.5 %copy-start.36 = (f32[8,32,32]{2,1,0:T(8,128)S(1)}, f32[8,32,32]{2,1,0:T(8,128)}, u32[]{:S(2)}) copy-start(f32[8,32,32]{2,1,0:T(8,128)} %copy-done.35) | copy-start | bytes 98308
  (33 other events, 51.4 us)
Sparse Core Ops, SparseCore 0:
  208.2 149.6 all-reduce.3
where the time goes:
time: 376 us; the launch traced here: 370 us
  blocking collectives  197 us (52%)
  waiting for transfers between devices  69.1 us (18%)
  matrix products  54.2 us (14%)
  local copies, waits for them, and re-layouts  22.5 us (6%)
  between operations  15.2 us (4%)
  other arithmetic  11.5 us (3%)
    psum x1, blocking collectives, local(): numerator_sums, denom = lax.psum((numerator_sums, denom), ('pts', 'grp'))  70 us
    psum x1, waiting for transfers between devices, local(): lax.psum(jnp.concatenate([rows_of(normed, d_mid), rows_of(normed, feature...  69.1 us
    psum x1, blocking collectives, local(): lax.psum((d_slice, d_temp, d_gain_one, d_gain_two), ('pts', 'grp'))  64.4 us
    psum x1, blocking collectives, local(): mixed_gradient = lax.psum(mixed_gradient, ('pts', 'grp'))  63.1 us
    unnamed x131, local copies, waits for them, and re-layouts  12.2 us
    dot_general x5, matrix products, transposed(): lax.dot_general(left, right, (((0,), (0,)), ((), ())), preferred_element_...  10.6 us
  transfers between devices with their start and end apart: 1, of which 1 were waited for; matrix products, arithmetic and copies ran while one was open for 4% of the time, Pallas kernels for 0%

commit v1 on v0

v1 whole, which is shorter than its diff:
```python
import jax
import jax.numpy as jnp
from jax import lax
from jax.experimental import pallas as pl
from jax.experimental.pallas import tpu as pltpu
from jax.sharding import PartitionSpec as P

F32 = jnp.float32
BF = jnp.bfloat16
MESH = pl.DeviceIdType.MESH
EXACT = lax.Precision.HIGHEST
C = 256
HEADS = 8
FF = 1024
NB = 512
EPS = 1e-5
K0 = 0.7978845608028654
K1 = K0 * 0.044715
ROWS_S = 72
PART_S = 24
ROWS_G = 4608
ROWS_T = 1152


def dg(a, b, ca, cb, precision=None):
    return lax.dot_general(
        a, b, (((ca,), (cb,)), ((), ())), precision=precision, preferred_element_type=F32
    )


def split3(v):
    hi = v.astype(BF)
    rest = v - hi.astype(F32)
    mid = rest.astype(BF)
    low = (rest - mid.astype(F32)).astype(BF)
    return hi, mid, low


def split2(v):
    hi = v.astype(BF)
    return hi, (v - hi.astype(F32)).astype(BF)


def iota(shape, dim):
    return lax.broadcasted_iota(jnp.int32, shape, dim)


def same_block(rows, cols):
    return (iota((rows, cols), 0) // 32) == (iota((rows, cols), 1) // 32)


def one_hot_rows(rows):
    return ((iota((rows, 32), 0) % 32) == iota((rows, 32), 1)).astype(F32)


def lanes4(col):
    return jnp.concatenate([col] * (NB // 128), axis=1)


def fold_lanes(v):
    out = v[:, 0:128]
    for j in range(1, v.shape[1] // 128):
        out = out + v[:, 128 * j : 128 * (j + 1)]
    return out


def column_to_rows(col):
    eye = iota((128, 128), 0) == iota((128, 128), 1)
    rows = []
    for a in range(col.shape[0] // 128):
        spread = jnp.broadcast_to(col[128 * a : 128 * (a + 1)], (128, 128))
        rows.append(jnp.sum(jnp.where(eye, spread, 0.0), axis=0, keepdims=True))
    return rows


def fold_diagonal(full):
    parts = []
    mask = same_block(128, 128)
    for a in range(2):
        sub = jnp.where(mask, full[128 * a : 128 * (a + 1), 128 * a : 128 * (a + 1)], 0.0)
        parts.append(sub[0:32] + sub[32:64] + sub[64:96] + sub[96:128])
    return jnp.concatenate(parts, axis=0)


def tile_diagonal(compact):
    return jnp.where(same_block(128, 128), jnp.concatenate([compact] * 4, axis=0), 0.0)


class Net:
    def __init__(self, send_sems, recv_sems, active):
        self.send_sems, self.recv_sems, self.active = send_sems, recv_sems, active
        self.count, self.open = 0, []
        if active:
            pts, z = lax.axis_index("pts"), lax.axis_index("grp")
            core, y, x = pts % 2, (pts // 2) % 4, pts // 8
            self.core = core
            self.at = (x, y, z)
            self.partner = (pts + 1 - 2 * core, z)
            self.peer = (
                lambda j: (j * 8 + y * 2 + core, z),
                lambda j: (x * 8 + j * 2 + core, z),
                lambda j: (pts, j),
            )

    def hello(self):
        if not self.active:
            return
        barrier = pltpu.get_barrier_semaphore()
        pl.semaphore_signal(barrier, inc=1, device_id=self.partner, device_id_type=MESH)
        for ax in range(3):
            for d in range(1, 4):
                pl.semaphore_signal(
                    barrier,
                    inc=1,
                    device_id=self.peer[ax]((self.at[ax] + d) % 4),
                    device_id_type=MESH,
                )

    def ready(self):
        if self.active:
            pl.semaphore_wait(pltpu.get_barrier_semaphore(), 10)

    def send(self, src, dst, device):
        k = self.count
        self.count += 1
        copy = pltpu.make_async_remote_copy(
            src_ref=src,
            dst_ref=dst,
            send_sem=self.send_sems.at[k],
            recv_sem=self.recv_sems.at[k],
            device_id=device,
            device_id_type=MESH,
        )
        copy.start()
        self.open.append(copy)
        return copy

    def drain(self):
        for copy in self.open:
            copy.wait_send()
        self.open = []


def rows(start, size):
    return pl.ds(pl.multiple_of(start, 8), size)


def small_sum(net, src, from_core, slots, out):
    if not net.active:
        out[...] = src[...]
        return
    copy = net.send(src, from_core, net.partner)
    yield
    copy.wait_recv()
    parts = [
        src[PART_S * p : PART_S * (p + 1), :] + from_core[PART_S * p : PART_S * (p + 1), :]
        for p in range(3)
    ]
    for k in range(3):
        copies = []
        for p in range(3):
            ax = (p + k) % 3
            mine = rows(k * 12 * PART_S + (p * 4 + net.at[ax]) * PART_S, PART_S)
            slots[mine, :] = parts[p]
            for d in range(1, 4):
                copies.append(
                    net.send(slots.at[mine, :], slots.at[mine, :], net.peer[ax]((net.at[ax] + d) % 4))
                )
        yield
        for copy in copies:
            copy.wait_recv()
        for p in range(3):
            four = [
                slots[pl.ds(k * 12 * PART_S + (p * 4 + s) * PART_S, PART_S), :]
                for s in range(4)
            ]
            parts[p] = (four[0] + four[1]) + (four[2] + four[3])
    for p in range(3):
        out[PART_S * p : PART_S * (p + 1), :] = parts[p]


def core_scatter(net, src, got, summed, part, barrier_copies=None):
    half = part // 2
    copies = []
    for p in range(3):
        theirs = rows(p * part + (1 - net.core) * half, half)
        copies.append(net.send(src.at[theirs, :], got.at[pl.ds(p * half, half), :], net.partner))
    yield
    for p, copy in enumerate(copies):
        copy.wait_recv()
        here = pl.ds(p * half, half)
        summed[here, :] = src[rows(p * part + net.core * half, half), :] + got[here, :]


def axis_scatter(net, k, src, got, size, store):
    piece = size // 4
    copies = []
    for p in range(3):
        ax = (p + k) % 3
        for d in range(1, 4):
            j = (net.at[ax] + d) % 4
            copies.append(
                net.send(
                    src.at[rows(p * size + j * piece, piece), :],
                    got.at[pl.ds((p * 3 + d - 1) * piece, piece), :],
                    net.peer[ax](j),
                )
            )
    yield
    for copy in copies:
        copy.wait_recv()
    for p in range(3):
        ax = (p + k) % 3
        own = src[rows(p * size + net.at[ax] * piece, piece), :]
        three = [got[pl.ds((p * 3 + d) * piece, piece), :] for d in range(3)]
        store(p, (own + three[0]) + (three[1] + three[2]))


def axis_exchange(net, k, slots, size, store):
    copies = []
    for p in range(3):
        ax = (p + k) % 3
        mine = rows((p * 4 + net.at[ax]) * size, size)
        for d in range(1, 4):
            copies.append(
                net.send(slots.at[mine, :], slots.at[mine, :], net.peer[ax]((net.at[ax] + d) % 4))
            )
    yield
    for copy in copies:
        copy.wait_recv()
    for p in range(3):
        four = [slots[pl.ds((p * 4 + s) * size, size), :] for s in range(4)]
        store(p, (four[0] + four[1]) + (four[2] + four[3]))


def axis_gather(net, k, out, where):
    copies = []
    for p in range(3):
        ax = (p + k) % 3
        for d in range(1, 4):
            here = out.at[where(p), :]
            copies.append(net.send(here, here, net.peer[ax]((net.at[ax] + d) % 4)))
    yield
    for copy in copies:
        copy.wait_recv()


def core_gather(net, out, where):
    copies = [net.send(out.at[where(p), :], out.at[where(p), :], net.partner) for p in range(3)]
    yield
    for copy in copies:
        copy.wait_recv()


def bulk_sum(net, src, got0, sum0, got1, sum1, got2, slots, out):
    if not net.active:
        out[...] = src[...]
        return
    part, half, quarter, piece = 1536, 768, 192, 48
    yield from core_scatter(net, src, got0, sum0, part)

    def keep1(p, v):
        sum1[pl.ds(p * quarter, quarter), :] = v

    yield from axis_scatter(net, 0, sum0, got1, half, keep1)

    def keep2(p, v):
        slots[rows((p * 4 + net.at[(p + 2) % 3]) * piece, piece), :] = v

    yield from axis_scatter(net, 1, sum1, got2, quarter, keep2)

    def base(p, depth):
        at = p * part + net.core * half
        if depth > 0:
            at = at + net.at[p % 3] * quarter
        if depth > 1:
            at = at + net.at[(p + 1) % 3] * piece
        return at

    def keep3(p, v):
        out[rows(base(p, 2), piece), :] = v

    yield from axis_exchange(net, 2, slots, piece, keep3)
    yield from axis_gather(net, 1, out, lambda p: rows(base(p, 2), piece))
    yield from axis_gather(net, 0, out, lambda p: rows(base(p, 1), quarter))
    yield from core_gather(net, out, lambda p: rows(base(p, 0), half))


def tail_sum(net, src, got0, sum0, got1, slots1, slots2, out):
    if not net.active:
        out[...] = src[...]
        return
    part, half, piece = 384, 192, 48
    yield from core_scatter(net, src, got0, sum0, part)

    def keep(slots, k):
        def store(p, v):
            slots[rows((p * 4 + net.at[(p + k) % 3]) * piece, piece), :] = v

        return store

    yield from axis_scatter(net, 0, sum0, got1, half, keep(slots1, 1))
    yield from axis_exchange(net, 1, slots1, piece, keep(slots2, 2))

    def where(p, depth):
        at = p * part + net.core * half
        if depth > 0:
            at = at + net.at[p % 3] * piece
        return rows(at, piece if depth else half)

    def last(p, v):
        out[where(p, 1), :] = v

    yield from axis_exchange(net, 2, slots2, piece, last)
    yield from axis_gather(net, 0, out, lambda p: where(p, 1))
    yield from core_gather(net, out, lambda p: where(p, 0))


def step_of(gen):
    next(gen, None)


def finish_of(gen):
    for _ in gen:
        pass


def kernel(
    active,
    points_h, cot_h, w_mid_h, w_feat_h, w_out_h, w_up_h, w_down_h,
    gain_one, gain_two, w_slice, w_temp, w_q, w_k, w_v,
    o_points, o_mid, o_feat, o_out, o_up, o_down,
    o_one, o_two, o_slice, o_temp, o_q, o_k, o_v,
    pts_v, cot_v, wm_v, wf_v, wo_v, wu_v, wd_v,
    pT, cT, wmfT, wmf, woT, wuT, wdT,
    g1c, g2c, wtc, bds, bdd, bqkv,
    stat, nT, mfT, rts, sgs, ls, ws, wb, dacc,
    tok_s, qkv_s, prob_s, denb_s, mixT, lhs_c, dnT, ddc,
    dhT, sT, n2T, xh2, hT, dpT, drT, drb, dsT, ga1, ga2,
    dl_s, dt_s, dmf_s, gp_v,
    s1_src, s1_core, s1_slots, s1_out, s2_src, s2_core, s2_slots, s2_out,
    b_src, b_got0, b_sum0, b_got1, b_sum1, b_got2, b_slots, b_out,
    t_src, t_got0, t_sum0, t_got1, t_slots1, t_slots2, t_out,
    in_sems, out_sems, send_sems, recv_sems,
):
    n = pts_v.shape[0]
    chunks = n // NB
    net = Net(send_sems, recv_sems, active)
    net.hello()

    loads = [
        pltpu.make_async_copy(src, dst, in_sems.at[i])
        for i, (src, dst) in enumerate(
            [(w_mid_h, wm_v), (w_feat_h, wf_v), (points_h, pts_v), (cot_h, cot_v),
             (w_out_h, wo_v), (w_up_h, wu_v), (w_down_h, wd_v)]
        )
    ]
    for load in loads:
        load.start()

    hot = one_hot_rows(256)
    mask = same_block(256, 256)
    slice_t = jnp.where(mask, dg(dg(hot, w_slice[...], 1, 1, EXACT), hot, 1, 1, EXACT), 0.0)
    slice_n = jnp.where(mask, dg(dg(hot, w_slice[...], 1, 0, EXACT), hot, 1, 1, EXACT), 0.0)
    temp8 = jnp.where(
        iota((8, 256), 0) == iota((8, 256), 1) // 32,
        dg(jnp.broadcast_to(w_temp[...], (8, 32)), hot, 1, 1, EXACT),
        0.0,
    )
    wtc[...] = dg(hot, jnp.broadcast_to(w_temp[...], (128, 32)), 1, 1, EXACT)
    for i, v in enumerate(split3(slice_t)):
        bds[256 * i : 256 * (i + 1), :] = v
    t_hi = temp8.astype(BF).astype(F32)
    t_mid = (temp8 - t_hi).astype(BF).astype(F32)
    t_low = temp8 - t_hi - t_mid
    bds[768:800, :] = jnp.concatenate([t_hi, t_mid, t_low, jnp.zeros((8, 256), F32)], axis=0).astype(BF)
    n_hi, n_lo = split2(slice_n)
    bdd[:, 0:256] = n_hi
    bdd[:, 256:512] = n_hi
    bdd[:, 512:768] = n_lo
    g1c[...] = jnp.broadcast_to(gain_one[...], (128, 256)).T
    g2c[...] = jnp.broadcast_to(gain_two[...], (128, 256)).T
    hot4 = one_hot_rows(128)
    mask4 = same_block(128, 128)
    for i, w in enumerate((w_q, w_k, w_v)):
        bqkv[:, 128 * i : 128 * (i + 1)] = jnp.where(
            mask4, dg(dg(hot4, w[...], 1, 0, EXACT), hot4, 1, 1, EXACT), 0.0
        )
    dacc[...] = jnp.zeros_like(dacc)
    ga1[...] = jnp.zeros_like(ga1)
    ga2[...] = jnp.zeros_like(ga2)
    t_src[1024:ROWS_T, :] = jnp.zeros((ROWS_T - 1024, 128), F32)

    loads[0].wait()
    loads[1].wait()
    wmfT[0:256, :] = wm_v[...].T
    wmfT[256:512, :] = wf_v[...].T
    wmf[:, 0:256] = wm_v[...]
    wmf[:, 256:512] = wf_v[...]
    loads[2].wait()

    def front(i, _):
        s = pl.ds(pl.multiple_of(i * NB, NB), NB)
        xT = pts_v[s, :].T
        pT[:, s] = xT
        x = xT.astype(F32)
        mean = jnp.sum(x, axis=0, keepdims=True) * (1.0 / C)
        xc = x - mean
        var = jnp.sum(xc * xc, axis=0, keepdims=True) * (1.0 / C)
        rstd = lax.rsqrt(var + EPS)
        stat[0:1, s] = mean
        stat[1:2, s] = rstd
        normed = (xc * rstd * lanes4(g1c[...])).astype(BF)
        nT[:, s] = normed
        mf = dg(wmfT[...], normed, 1, 0).astype(BF)
        mfT[:, s] = mf
        lg = dg(bds[...], mf[0:256], 1, 0)
        t = lg[768:776] + lg[776:784] + lg[784:792]
        rt = 1.0 / (0.5 + (jnp.maximum(t, 0.0) + jnp.log(1.0 + jnp.exp(-jnp.abs(t)))))
        rts[:, s] = rt
        sgs[:, s] = 1.0 / (1.0 + jnp.exp(-t))
        for h in range(HEADS):
            r = slice(32 * h, 32 * h + 32)
            l = (lg[r] + lg[256 + 32 * h : 288 + 32 * h] + lg[512 + 32 * h : 544 + 32 * h]) * rt[h : h + 1]
            e = jnp.exp(l - jnp.max(l, axis=0, keepdims=True))
            w = e * (1.0 / jnp.sum(e, axis=0, keepdims=True))
            ls[r, s] = l
            ws[r, s] = w
            wb[r, s] = w.astype(BF)
            dacc[r, :] += fold_lanes(w)
        return 0

    lax.fori_loop(0, chunks, front, 0)
    s1_src[0:64, :] = fold_diagonal(dg(wb[...], mfT[256:512, :], 1, 1))
    den_rows = column_to_rows(jnp.sum(dacc[...], axis=1, keepdims=True))
    s1_src[64:72, :] = jnp.concatenate(den_rows + [jnp.zeros((6, 128), F32)], axis=0)

    net.ready()
    first = small_sum(net, s1_src, s1_core, s1_slots, s1_out)
    step_of(first)

    for i in range(3, 7):
        loads[i].wait()
    wdT[...] = wd_v[...].T

    def hidden_gradient(i):
        s = pl.ds(pl.multiple_of(i * NB, NB), NB)
        cT[:, s] = cot_v[s, :].T
        dhT[:, s] = dg(wdT[...], cT[:, s], 1, 0)

    for i in range(chunks):
        hidden_gradient(i)
        if i == 0:
            woT[...] = wo_v[...].T
            wuT[...] = wu_v[...].T
        step_of(first)
    finish_of(first)

    total = s1_out[0:64, :]
    picked = []
    pick = (iota((32, 128), 1) % 32) == iota((32, 128), 0)
    for a in range(2):
        picked.append(jnp.where(pick, jnp.broadcast_to(s1_out[64 + a : 65 + a, :], (32, 128)), 0.0))
    ones4 = mask4.astype(F32)
    denb = dg(jnp.concatenate(picked, axis=0), ones4, 1, 0, EXACT) + EPS
    denb_s[...] = denb
    tok = total / denb
    tok_s[...] = tok
    qkv = dg(tok, bqkv[...], 1, 0, EXACT)
    qkv_s[...] = qkv
    scale = 32.0 ** (-0.5)
    mixT[...] = jnp.zeros_like(mixT)
    lhs_c[...] = jnp.zeros_like(lhs_c)
    for a in range(2):
        r = slice(32 * a, 32 * a + 32)
        q_a, k_a, v_a = qkv[r, 0:128], qkv[r, 128:256], qkv[r, 256:384]
        sc = dg(k_a, tile_diagonal(q_a), 1, 1, EXACT) * scale
        e = jnp.exp(sc - jnp.max(sc, axis=0, keepdims=True))
        pr = e / jnp.sum(e, axis=0, keepdims=True)
        prob_s[r, :] = pr
        m_t = jnp.where(mask4, dg(v_a, pr, 0, 0, EXACT), 0.0)
        block = slice(128 * a, 128 * a + 128)
        mixT[block, block] = m_t.astype(BF)
        lhs_c[block, block] = m_t.T.astype(BF)

    def rear(i, _):
        s = pl.ds(pl.multiple_of(i * NB, NB), NB)
        sp = dg(mixT[...], wb[:, s], 1, 0).astype(BF)
        sT[:, s] = sp
        res = (pT[:, s].astype(F32) + dg(woT[...], sp, 1, 0)).astype(BF).astype(F32)
        xc = res - jnp.sum(res, axis=0, keepdims=True) * (1.0 / C)
        var = jnp.sum(xc * xc, axis=0, keepdims=True) * (1.0 / C)
        rstd = lax.rsqrt(var + EPS)
        xhat = xc * rstd
        xh2[...] = xhat
        n2 = (xhat * lanes4(g2c[...])).astype(BF)
        n2T[:, s] = n2
        for f in range(FF // 256):
            fr = slice(256 * f, 256 * f + 256)
            pre = dg(wuT[fr, :], n2, 1, 0)
            x2 = pre * pre
            h = 0.5 + 0.5 * jnp.tanh(pre * (K0 + K1 * x2))
            hT[fr, s] = (pre * h).astype(BF)
            slope = h + (pre * (2.0 * K0 + (6.0 * K1) * x2)) * (h - h * h)
            dpT[fr, s] = (dhT[fr, s] * slope).astype(BF)
        dy = dg(wu_v[...], dpT[:, s], 1, 0)
        xhat = xh2[...]
        ga2[...] += fold_lanes(dy * xhat)
        dx = dy * lanes4(g2c[...])
        m1 = jnp.sum(dx, axis=0, keepdims=True) * (1.0 / C)
        m2 = jnp.sum(dx * xhat, axis=0, keepdims=True) * (1.0 / C)
        dr = cT[:, s].astype(F32) + rstd * (dx - m1 - xhat * m2)
        drT[:, s] = dr
        low = dr.astype(BF)
        drb[:, s] = low
        dsT[:, s] = dg(wo_v[...], low, 1, 0).astype(BF)
        return 0

    lax.fori_loop(0, chunks, rear, 0)
    s2_src[0:64, :] = fold_diagonal(dg(wb[...], dsT[...], 1, 1))
    s2_src[64:72, :] = jnp.zeros((8, 128), F32)
    second = small_sum(net, s2_src, s2_core, s2_slots, s2_out)
    step_of(second)

    def put(left, right, at):
        v = dg(left, right, 1, 1)
        for j in range(v.shape[1] // 128):
            b_src[256 * (at + j) : 256 * (at + j + 1), :] = v[:, 128 * j : 128 * (j + 1)]

    bulk = bulk_sum(net, b_src, b_got0, b_sum0, b_got1, b_sum1, b_got2, b_slots, b_out)
    for f in range(4):
        fr = slice(256 * f, 256 * f + 256)
        put(n2T[...], dpT[fr, :], 2 * f)
        put(cT[...], hT[fr, :], 8 + 2 * f)
        if f == 3:
            put(sT[...], drb[...], 16)
        else:
            step_of(second)
    finish_of(second)
    step_of(bulk)

    dqs, dks, dvs = [], [], []
    for a in range(2):
        r = slice(32 * a, 32 * a + 32)
        q_a, k_a, v_a = qkv_s[r, 0:128], qkv_s[r, 128:256], qkv_s[r, 256:384]
        pr = prob_s[r, :]
        d_bd = tile_diagonal(s2_out[r, :])
        dvs.append(dg(pr, d_bd, 1, 0, EXACT))
        dp = dg(v_a, d_bd, 1, 1, EXACT)
        dsc = pr * (dp - jnp.sum(pr * dp, axis=0, keepdims=True)) * scale
        dq = jnp.where(mask4, dg(dsc, k_a, 0, 0, EXACT), 0.0)
        dqs.append(dq[0:32] + dq[32:64] + dq[64:96] + dq[96:128])
        dks.append(dg(dsc, tile_diagonal(q_a), 1, 0, EXACT))
    d_all = jnp.concatenate(
        [jnp.concatenate(v, axis=0) for v in (dqs, dks, dvs)], axis=1
    )
    d_tok = dg(d_all, bqkv[...], 1, 1, EXACT)
    tok = tok_s[...]
    d_num = d_tok / denb_s[...]
    d_den = -(d_num * tok)
    for a in range(2):
        r = slice(32 * a, 32 * a + 32)
        block = slice(128 * a, 128 * a + 128)
        bd = tile_diagonal(d_num[r])
        hi, lo = split2(bd)
        lhs_c[block, 256 + 128 * a : 384 + 128 * a] = hi
        lhs_c[block, 512 + 128 * a : 640 + 128 * a] = lo
        ddc[block, :] = jnp.broadcast_to(
            jnp.sum(tile_diagonal(d_den[r]), axis=1, keepdims=True), (128, 128)
        )
        hi_t, lo_t = split2(bd.T)
        dnT[block, :] = jnp.zeros((128, 512), BF)
        dnT[block, block] = hi_t
        dnT[block, 256 + 128 * a : 384 + 128 * a] = lo_t

    def finish(i):
        s = pl.ds(pl.multiple_of(i * NB, NB), NB)
        feats = mfT[256:512, s]
        dw = dg(lhs_c[...], jnp.concatenate([dsT[:, s], feats, feats], axis=0), 1, 0)
        sg, rt = sgs[:, s], rts[:, s]
        dts = []
        for h in range(HEADS):
            r = slice(32 * h, 32 * h + 32)
            w = ws[r, s]
            g = dw[r] + lanes4(ddc[r, :])
            d_l = w * (g - jnp.sum(w * g, axis=0, keepdims=True))
            inner = jnp.sum(d_l * ls[r, s], axis=0, keepdims=True)
            scale_h = rt[h : h + 1]
            dts.append(-(inner * scale_h) * sg[h : h + 1])
            hi, lo = split2(d_l * scale_h)
            dl_s[r, s] = hi
            dl_s[256 + 32 * h : 288 + 32 * h, s] = lo
        dt = jnp.concatenate(dts, axis=0)
        dt_hi = dt.astype(BF).astype(F32)
        dt_s[:, s] = jnp.concatenate([dt_hi, dt - dt_hi], axis=0).astype(BF)
        hi = dl_s[0:256, s]
        dm = dg(bdd[...], jnp.concatenate([hi, dl_s[256:512, s], hi], axis=0), 1, 0)
        for h in range(HEADS):
            r = slice(32 * h, 32 * h + 32)
            dmf_s[r, s] = (dm[r] + lanes4(wtc[r, :]) * dt[h : h + 1]).astype(BF)
        wbs = wb[:, s]
        dmf_s[256:512, s] = dg(dnT[...], jnp.concatenate([wbs, wbs], axis=0), 1, 0).astype(BF)
        dy = dg(wmf[...], dmf_s[:, s], 1, 0)
        rstd = stat[1:2, s]
        xhat = (pT[:, s].astype(F32) - stat[0:1, s]) * rstd
        ga1[...] += fold_lanes(dy * xhat)
        dx = dy * lanes4(g1c[...])
        m1 = jnp.sum(dx, axis=0, keepdims=True) * (1.0 / C)
        m2 = jnp.sum(dx * xhat, axis=0, keepdims=True) * (1.0 / C)
        out = (drT[:, s] + rstd * (dx - m1 - xhat * m2)).astype(BF)
        gp_v[s, :] = out.T

    for i in range(chunks):
        finish(i)
        step_of(bulk)
    stores = [pltpu.make_async_copy(gp_v, o_points, out_sems.at[0])]
    stores[0].start()

    gmf = dg(nT[...], dmf_s[...], 1, 1)
    for j in range(4):
        t_src[256 * j : 256 * (j + 1), :] = gmf[:, 128 * j : 128 * (j + 1)]
    mids = mfT[0:256, :]
    gs = dg(mids, dl_s[0:256, :], 1, 1) + dg(mids, dl_s[256:512, :], 1, 1)
    gs64 = fold_diagonal(gs)
    t_src[1024:1056, :] = gs64[0:32] + gs64[32:64]
    gt = dg(mids, dt_s[...], 1, 1)
    gt = jnp.where(iota((256, 16), 1) % 8 == iota((256, 16), 0) // 32, gt, 0.0)
    gt = jnp.sum(gt, axis=1, keepdims=True)
    gt32 = gt[0:32]
    for h in range(1, HEADS):
        gt32 = gt32 + gt[32 * h : 32 * h + 32]
    t_src[1056:1088, :] = jnp.broadcast_to(gt32, (32, 128))
    gain_rows = column_to_rows(jnp.sum(ga1[...], axis=1, keepdims=True)) + column_to_rows(
        jnp.sum(ga2[...], axis=1, keepdims=True)
    )
    t_src[1088:1096, :] = jnp.concatenate(gain_rows + [jnp.zeros((4, 128), F32)], axis=0)

    tail = tail_sum(net, t_src, t_got0, t_sum0, t_got1, t_slots1, t_slots2, t_out)
    step_of(tail)

    for i, (o, d) in enumerate(((o_q, dqs), (o_k, dks), (o_v, dvs))):
        full = jnp.where(mask4, dg(tok, jnp.concatenate(d, axis=0), 0, 0, EXACT), 0.0)
        o[...] = dg(dg(hot4, full, 0, 0, EXACT), hot4, 1, 0, EXACT)

    for _ in range(8):
        step_of(bulk)
        step_of(tail)

    def store_columns(src, at, out, count, sem):
        for j in range(count):
            copy = pltpu.make_async_copy(
                src.at[pl.ds(256 * (at + j), 256), :],
                out.at[:, pl.ds(128 * j, 128)],
                out_sems.at[sem + j],
            )
            copy.start()
            stores.append(copy)

    store_columns(b_out, 0, o_up, 8, 1)
    store_columns(b_out, 8, o_down, 8, 9)
    store_columns(b_out, 16, o_out, 2, 17)
    finish_of(tail)
    store_columns(t_out, 0, o_mid, 2, 19)
    store_columns(t_out, 2, o_feat, 2, 21)
    o_slice[...] = dg(t_out[1024:1056, :], hot4, 1, 0, EXACT)
    diag = iota((32, 128), 0) == iota((32, 128), 1)
    o_temp[...] = jnp.sum(jnp.where(diag, t_out[1056:1088, :], 0.0), axis=0, keepdims=True)[:, 0:32]
    o_one[:, 0:128] = t_out[1088:1089, :]
    o_one[:, 128:256] = t_out[1089:1090, :]
    o_two[:, 0:128] = t_out[1090:1091, :]
    o_two[:, 128:256] = t_out[1091:1092, :]
    for store in stores:
        store.wait()
    net.drain()


def call(active, n, args):
    (points, cotangent, gain_one, gain_two, w_mid, w_feat, w_out, w_up, w_down,
     w_slice, w_temp, w_q, w_k, w_v) = args
    vm = lambda *shape: pltpu.VMEM(shape, F32)
    vb = lambda *shape: pltpu.VMEM(shape, BF)
    any_spec = pl.BlockSpec(memory_space=pl.ANY)
    vmem_spec = pl.BlockSpec(memory_space=pltpu.VMEM)
    out_shape = (
        [jax.ShapeDtypeStruct((n, C), BF)]
        + [jax.ShapeDtypeStruct((C, C), F32)] * 3
        + [jax.ShapeDtypeStruct((C, FF), F32)] * 2
        + [jax.ShapeDtypeStruct((1, C), F32)] * 2
        + [jax.ShapeDtypeStruct((32, 32), F32), jax.ShapeDtypeStruct((1, 32), F32)]
        + [jax.ShapeDtypeStruct((32, 32), F32)] * 3
    )
    small = [vm(ROWS_S, 128), vm(ROWS_S, 128), vm(36 * PART_S, 128), vm(ROWS_S, 128)]
    scratch = (
        [vb(n, C), vb(n, C), vb(C, C), vb(C, C), vb(C, C), vb(C, FF), vb(C, FF)]
        + [vb(C, n), vb(C, n), vb(512, C), vb(C, 512), vb(C, C), vb(FF, C), vb(FF, C)]
        + [vm(C, 128), vm(C, 128), vm(C, 128), vb(800, C), vb(C, 768), vm(128, 384)]
        + [vm(8, n), vb(C, n), vb(512, n), vm(8, n), vm(8, n), vm(C, n), vm(C, n), vb(C, n), vm(C, 128)]
        + [vm(64, 128), vm(64, 384), vm(64, 128), vm(64, 128), vb(C, C), vb(C, 768), vb(C, 512), vm(C, 128)]
        + [vm(FF, n), vb(C, n), vb(C, n), vm(C, NB), vb(FF, n), vb(FF, n), vm(C, n), vb(C, n), vb(C, n),
           vm(C, 128), vm(C, 128)]
        + [vb(512, n), vb(16, n), vb(512, n), vb(n, C)]
        + small
        + small
        + [vm(ROWS_G, 128), vm(2304, 128), vm(2304, 128), vm(9 * 192, 128), vm(576, 128), vm(9 * 48, 128),
           vm(12 * 48, 128), vm(ROWS_G, 128)]
        + [vm(ROWS_T, 128), vm(576, 128), vm(576, 128), vm(9 * 48, 128), vm(12 * 48, 128), vm(12 * 48, 128),
           vm(ROWS_T, 128)]
        + [pltpu.SemaphoreType.DMA((7,)), pltpu.SemaphoreType.DMA((23,)),
           pltpu.SemaphoreType.DMA((160,)), pltpu.SemaphoreType.DMA((160,))]
    )

    def body(*refs):
        kernel(active, *refs)

    outs = pl.pallas_call(
        body,
        name="block_backward",
        out_shape=out_shape,
        in_specs=[any_spec] * 7 + [vmem_spec] * 7,
        out_specs=[any_spec] * 6 + [vmem_spec] * 7,
        scratch_shapes=scratch,
        compiler_params=pltpu.CompilerParams(
            vmem_limit_bytes=62 * 2**20,
            has_side_effects=True,
            **({"collective_id": 0} if active else {}),
        ),
    )(
        points, cotangent, w_mid, w_feat, w_out, w_up, w_down,
        gain_one.reshape(1, C), gain_two.reshape(1, C), w_slice, w_temp.reshape(1, 32), w_q, w_k, w_v,
    )
    outs = list(outs)
    outs[6], outs[7], outs[9] = outs[6].reshape(C), outs[7].reshape(C), outs[9].reshape(32)
    return tuple(outs)


def solution(mesh):
    rows_spec = P(("pts", "grp"), None)

    def local(*args):
        return call(True, args[0].shape[0], args)

    return jax.shard_map(
        local,
        mesh=mesh,
        in_specs=(rows_spec, rows_spec) + (P(),) * 12,
        out_specs=(rows_spec,) + (P(),) * 12,
        check_vma=False,
    )
```

time: 376 us -> 110 us (0.29); the launches traced: 370 us -> 110 us
  blocking collectives: 197 us -> 0 us
  Pallas kernels: 0 us -> 97.6 us
  waiting for transfers between devices: 69.1 us -> 0 us
  matrix products: 54.2 us -> 0 us
  between operations: 15.2 us -> 0.7 us
  other arithmetic: 11.5 us -> 0 us
  local copies, waits for them, and re-layouts: 22.5 us -> 11.4 us
    psum x3 -> x0, blocking collectives: 197 us -> none  [the longest x1 70 us: local(): numerator_sums, denom = lax.psum((numerator_sums, denom), ('pts', 'grp'))]
    pallas_call x0 -> x1, Pallas kernels: none -> 97.6 us  [call(): pl.pallas_call(body, name='block_backward', out_shape=out_shape, in_specs...]
    psum x1 -> x0, waiting for transfers between devices: 69.1 us -> none  [local(): lax.psum(jnp.concatenate([rows_of(normed, d_mid), rows_of(normed, feature...]
    dot_general x40 -> x0, matrix products: 54.2 us -> none  [the longest x5 10.6 us: transposed(): lax.dot_general(left, right, (((0,), (0,)), ((), ())), preferred_element_...]
    reduce_sum x8 -> x0, other arithmetic: 5.71 us -> none  [the longest x2 3.52 us: layer_norm(): return centred * lax.rsqrt(spread_tokens + EPS_NORM) * gain]
    dot_general x1 -> x0, local copies, waits for them, and re-layouts: 5.21 us -> none  [assign(): jnp.einsum('nhd,d->nh', middle, w_temp, precision=PRECISION_LEVEL)]
    slice x2 -> x0, local copies, waits for them, and re-layouts: 5.11 us -> none  [the longest x1 3.11 us: local(): big[:, 3 * width + hidden_units:]]
    unnamed x131 -> x37, local copies, waits for them, and re-layouts: 12.2 us -> 11.4 us
  transfers between devices with their start and end apart: 1 -> 0, of which waited for: 1 -> 0; matrix products, arithmetic and copies ran while one was open for 4% -> 0% of each run, Pallas kernels for 0% -> 0%
where the time goes in v1:
time: 110 us
  Pallas kernels  97.6 us (89%)
  local copies, waits for them, and re-layouts  11.4 us (10%)
    pallas_call x1, Pallas kernels, call(): pl.pallas_call(body, name='block_backward', out_shape=out_shape, in_specs...  97.6 us
    unnamed x37, local copies, waits for them, and re-layouts  11.4 us

profile of v1, /device:TPU:1, one launch (start us, length us, event | category | flops | bytes accessed | tf_op | source)
XLA Modules:
  0.0 109.8 jit_solution(5359196955939765788)
XLA Ops:
  0.7 97.6 %block_backward.1 = (bf16[2048,256]{1,0:T(8,128)(2,1)}, f32[256,256]{1,0:T(8,128)}, f32[256,256]{1,0:T(8,128)}, f32[256,256]{1,0:T(8,128)}, f32[256,1024]{1,0:T(...) custom-call(bf16[2048,256]{1,0:T(8,128)(2,1)} %refs_0_.1, ...), custom_call_target="tpu_custom_call" | custom-call | tf_op jit(solution)/shard_map/block_backward/pallas_call | solution.py:715
  98.3 0.0 copy-start.4
  98.3 0.0 copy-start.3
  98.3 0.0 copy-start.2
  98.3 2.3 %copy.40 = bf16[2048,256]{1,0:T(8,128)(2,1)} copy(bf16[2048,256]{1,0:T(8,128)(2,1)} %get-tuple-element.52) | data formatting | bytes 2097152
  100.6 0.0 copy-done.4
  100.6 0.0 copy-start.1
  100.6 0.7 copy.41
  101.3 0.0 copy-done.3
  101.3 0.7 copy.42
  102.0 0.0 copy-done.2
  102.0 0.7 copy.43
  102.7 0.0 copy-done.1
  102.7 0.0 copy-start
  102.7 1.0 copy.44
  103.7 0.6 copy-done
  104.3 0.0 copy-start.10
  104.4 1.0 copy.45
  105.3 0.0 copy-done.10
  105.3 0.6 copy.46
  105.9 0.1 copy-done.9
  106.0 0.6 copy.47
  106.6 0.0 copy-done.8
  106.6 0.6 copy.48
  107.2 0.0 copy-done.11
  107.2 0.5 copy.49
  107.7 0.0 copy-done.7
  107.7 0.6 copy.50
  108.3 0.1 copy-done.6
  108.4 0.6 copy.51
  109.0 0.1 copy-done.5
  109.1 0.6 copy.52
  (6 shorter events, 0.0 us)
Async XLA Ops:
  98.3 2.4 %copy-start.4 = (f32[256,256]{1,0:T(8,128)S(1)}, f32[256,256]{1,0:T(8,128)}, u32[]{:S(2)}) copy-start(f32[256,256]{1,0:T(8,128)} %get-tuple-element.53) | copy-start | bytes 786436
  98.3 3.1 %copy-start.3 = (f32[256,256]{1,0:T(8,128)S(1)}, f32[256,256]{1,0:T(8,128)}, u32[]{:S(2)}) copy-start(f32[256,256]{1,0:T(8,128)} %get-tuple-element.54) | copy-start | bytes 786436
  98.3 3.8 %copy-start.2 = (f32[256,256]{1,0:T(8,128)S(1)}, f32[256,256]{1,0:T(8,128)}, u32[]{:S(2)}) copy-start(f32[256,256]{1,0:T(8,128)} %get-tuple-element.55) | copy-start | bytes 786436
  100.6 2.1 %copy-start.1 = (f32[256,1024]{1,0:T(8,128)S(1)}, f32[256,1024]{1,0:T(8,128)}, u32[]{:S(2)}) copy-start(f32[256,1024]{1,0:T(8,128)} %get-tuple-element.56) | copy-start | bytes 3145732
  102.7 1.6 %copy-start = (f32[256,1024]{1,0:T(8,128)S(1)}, f32[256,1024]{1,0:T(8,128)}, u32[]{:S(2)}) copy-start(f32[256,1024]{1,0:T(8,128)} %get-tuple-element.57) | copy-start | bytes 3145732
  104.3 1.0 copy-start.10
  104.4 2.2 %copy-start.8 = (f32[32,32]{1,0:T(8,128)S(1)}, f32[32,32]{1,0:T(8,128)}, u32[]{:S(2)}) copy-start(f32[32,32]{1,0:T(8,128)} %get-tuple-element.60) | copy-start | bytes 12292
  105.3 0.7 copy-start.9
  106.6 0.6 copy-start.11
  106.6 1.1 %copy-start.7 = (f32[32,32]{1,0:T(8,128)S(1)}, f32[32,32]{1,0:T(8,128)}, u32[]{:S(2)}) copy-start(f32[32,32]{1,0:T(8,128)} %get-tuple-element.62) | copy-start | bytes 12292
  107.7 0.7 copy-start.6
  108.4 0.7 copy-start.5

commit v2 on v1

--- a/solution.py
+++ b/solution.py
@@ -12,7 +12,7 @@
 C = 256
 HEADS = 8
 FF = 1024
-NB = 512
+NB = 1024
 EPS = 1e-5
 K0 = 0.7978845608028654
 K1 = K0 * 0.044715
@@ -329,19 +329,19 @@
     active,
     points_h, cot_h, w_mid_h, w_feat_h, w_out_h, w_up_h, w_down_h,
     gain_one, gain_two, w_slice, w_temp, w_q, w_k, w_v,
-    o_points, o_mid, o_feat, o_out, o_up, o_down,
-    o_one, o_two, o_slice, o_temp, o_q, o_k, o_v,
+    gp_v, b_out, t_out, o_small,
     pts_v, cot_v, wm_v, wf_v, wo_v, wu_v, wd_v,
     pT, cT, wmfT, wmf, woT, wuT, wdT,
     g1c, g2c, wtc, bds, bdd, bqkv,
     stat, nT, mfT, rts, sgs, ls, ws, wb, dacc,
     tok_s, qkv_s, prob_s, denb_s, mixT, lhs_c, dnT, ddc,
     dhT, sT, n2T, xh2, hT, dpT, drT, drb, dsT, ga1, ga2,
-    dl_s, dt_s, dmf_s, gp_v,
+    dl_s, dt_s, dmf_s,
     s1_src, s1_core, s1_slots, s1_out, s2_src, s2_core, s2_slots, s2_out,
-    b_src, b_got0, b_sum0, b_got1, b_sum1, b_got2, b_slots, b_out,
-    t_src, t_got0, t_sum0, t_got1, t_slots1, t_slots2, t_out,
-    in_sems, out_sems, send_sems, recv_sems,
+    s3_src, s3_core, s3_slots, s3_out,
+    b_src, b_got0, b_sum0, b_got1, b_sum1, b_got2, b_slots,
+    t_src, t_got0, t_sum0, t_got1, t_slots1, t_slots2,
+    in_sems, send_sems, recv_sems,
 ):
     n = pts_v.shape[0]
     chunks = n // NB
@@ -361,31 +361,18 @@
     hot = one_hot_rows(256)
     mask = same_block(256, 256)
     slice_t = jnp.where(mask, dg(dg(hot, w_slice[...], 1, 1, EXACT), hot, 1, 1, EXACT), 0.0)
-    slice_n = jnp.where(mask, dg(dg(hot, w_slice[...], 1, 0, EXACT), hot, 1, 1, EXACT), 0.0)
     temp8 = jnp.where(
         iota((8, 256), 0) == iota((8, 256), 1) // 32,
         dg(jnp.broadcast_to(w_temp[...], (8, 32)), hot, 1, 1, EXACT),
         0.0,
     )
-    wtc[...] = dg(hot, jnp.broadcast_to(w_temp[...], (128, 32)), 1, 1, EXACT)
     for i, v in enumerate(split3(slice_t)):
         bds[256 * i : 256 * (i + 1), :] = v
     t_hi = temp8.astype(BF).astype(F32)
     t_mid = (temp8 - t_hi).astype(BF).astype(F32)
     t_low = temp8 - t_hi - t_mid
     bds[768:800, :] = jnp.concatenate([t_hi, t_mid, t_low, jnp.zeros((8, 256), F32)], axis=0).astype(BF)
-    n_hi, n_lo = split2(slice_n)
-    bdd[:, 0:256] = n_hi
-    bdd[:, 256:512] = n_hi
-    bdd[:, 512:768] = n_lo
     g1c[...] = jnp.broadcast_to(gain_one[...], (128, 256)).T
-    g2c[...] = jnp.broadcast_to(gain_two[...], (128, 256)).T
-    hot4 = one_hot_rows(128)
-    mask4 = same_block(128, 128)
-    for i, w in enumerate((w_q, w_k, w_v)):
-        bqkv[:, 128 * i : 128 * (i + 1)] = jnp.where(
-            mask4, dg(dg(hot4, w[...], 1, 0, EXACT), hot4, 1, 1, EXACT), 0.0
-        )
     dacc[...] = jnp.zeros_like(dacc)
     ga1[...] = jnp.zeros_like(ga1)
     ga2[...] = jnp.zeros_like(ga2)
@@ -430,7 +417,8 @@
             dacc[r, :] += fold_lanes(w)
         return 0
 
-    lax.fori_loop(0, chunks, front, 0)
+    for i in range(chunks):
+        front(i, 0)
     s1_src[0:64, :] = fold_diagonal(dg(wb[...], mfT[256:512, :], 1, 1))
     den_rows = column_to_rows(jnp.sum(dacc[...], axis=1, keepdims=True))
     s1_src[64:72, :] = jnp.concatenate(den_rows + [jnp.zeros((6, 128), F32)], axis=0)
@@ -439,6 +427,19 @@
     first = small_sum(net, s1_src, s1_core, s1_slots, s1_out)
     step_of(first)
 
+    slice_n = jnp.where(mask, dg(dg(hot, w_slice[...], 1, 0, EXACT), hot, 1, 1, EXACT), 0.0)
+    n_hi, n_lo = split2(slice_n)
+    bdd[:, 0:256] = n_hi
+    bdd[:, 256:512] = n_hi
+    bdd[:, 512:768] = n_lo
+    wtc[...] = dg(hot, jnp.broadcast_to(w_temp[...], (128, 32)), 1, 1, EXACT)
+    g2c[...] = jnp.broadcast_to(gain_two[...], (128, 256)).T
+    hot4 = one_hot_rows(128)
+    mask4 = same_block(128, 128)
+    for i, w in enumerate((w_q, w_k, w_v)):
+        bqkv[:, 128 * i : 128 * (i + 1)] = jnp.where(
+            mask4, dg(dg(hot4, w[...], 1, 0, EXACT), hot4, 1, 1, EXACT), 0.0
+        )
     for i in range(3, 7):
         loads[i].wait()
     wdT[...] = wd_v[...].T
@@ -448,12 +449,12 @@
         cT[:, s] = cot_v[s, :].T
         dhT[:, s] = dg(wdT[...], cT[:, s], 1, 0)
 
-    for i in range(chunks):
+    hidden_gradient(0)
+    step_of(first)
+    for i in range(1, chunks):
         hidden_gradient(i)
-        if i == 0:
-            woT[...] = wo_v[...].T
-            wuT[...] = wu_v[...].T
-        step_of(first)
+    woT[...] = wo_v[...].T
+    wuT[...] = wu_v[...].T
     finish_of(first)
 
     total = s1_out[0:64, :]
@@ -516,7 +517,8 @@
         dsT[:, s] = dg(wo_v[...], low, 1, 0).astype(BF)
         return 0
 
-    lax.fori_loop(0, chunks, rear, 0)
+    for i in range(chunks):
+        rear(i, 0)
     s2_src[0:64, :] = fold_diagonal(dg(wb[...], dsT[...], 1, 1))
     s2_src[64:72, :] = jnp.zeros((8, 128), F32)
     second = small_sum(net, s2_src, s2_core, s2_slots, s2_out)
@@ -532,12 +534,14 @@
         fr = slice(256 * f, 256 * f + 256)
         put(n2T[...], dpT[fr, :], 2 * f)
         put(cT[...], hT[fr, :], 8 + 2 * f)
-        if f == 3:
-            put(sT[...], drb[...], 16)
-        else:
+        if f == 1:
             step_of(second)
+    put(sT[...], drb[...], 16)
+    step_of(bulk)
+    step_of(second)
+    step_of(bulk)
+    step_of(second)
     finish_of(second)
-    step_of(bulk)
 
     dqs, dks, dvs = [], [], []
     for a in range(2):
@@ -600,6 +604,9 @@
             dmf_s[r, s] = (dm[r] + lanes4(wtc[r, :]) * dt[h : h + 1]).astype(BF)
         wbs = wb[:, s]
         dmf_s[256:512, s] = dg(dnT[...], jnp.concatenate([wbs, wbs], axis=0), 1, 0).astype(BF)
+
+    def points_gradient(i):
+        s = pl.ds(pl.multiple_of(i * NB, NB), NB)
         dy = dg(wmf[...], dmf_s[:, s], 1, 0)
         rstd = stat[1:2, s]
         xhat = (pT[:, s].astype(F32) - stat[0:1, s]) * rstd
@@ -613,8 +620,6 @@
     for i in range(chunks):
         finish(i)
         step_of(bulk)
-    stores = [pltpu.make_async_copy(gp_v, o_points, out_sems.at[0])]
-    stores[0].start()
 
     gmf = dg(nT[...], dmf_s[...], 1, 1)
     for j in range(4):
@@ -630,48 +635,71 @@
     for h in range(1, HEADS):
         gt32 = gt32 + gt[32 * h : 32 * h + 32]
     t_src[1056:1088, :] = jnp.broadcast_to(gt32, (32, 128))
+    tail = tail_sum(net, t_src, t_got0, t_sum0, t_got1, t_slots1, t_slots2, t_out)
+    step_of(tail)
+    points_gradient(0)
+    step_of(tail)
+    for i in range(1, chunks):
+        points_gradient(i)
     gain_rows = column_to_rows(jnp.sum(ga1[...], axis=1, keepdims=True)) + column_to_rows(
         jnp.sum(ga2[...], axis=1, keepdims=True)
     )
-    t_src[1088:1096, :] = jnp.concatenate(gain_rows + [jnp.zeros((4, 128), F32)], axis=0)
-
-    tail = tail_sum(net, t_src, t_got0, t_sum0, t_got1, t_slots1, t_slots2, t_out)
-    step_of(tail)
-
-    for i, (o, d) in enumerate(((o_q, dqs), (o_k, dks), (o_v, dvs))):
+    s3_src[0:8, :] = jnp.concatenate(gain_rows + [jnp.zeros((4, 128), F32)], axis=0)
+    s3_src[8:ROWS_S, :] = jnp.zeros((ROWS_S - 8, 128), F32)
+    third = small_sum(net, s3_src, s3_core, s3_slots, s3_out)
+    step_of(third)
+    step_of(bulk)
+    step_of(third)
+
+    for i, d in enumerate((dqs, dks, dvs)):
         full = jnp.where(mask4, dg(tok, jnp.concatenate(d, axis=0), 0, 0, EXACT), 0.0)
-        o[...] = dg(dg(hot4, full, 0, 0, EXACT), hot4, 1, 0, EXACT)
+        o_small[32 * i : 32 * (i + 1), :] = dg(hot4, full, 0, 0, EXACT)
 
     for _ in range(8):
+        step_of(tail)
         step_of(bulk)
-        step_of(tail)
+        step_of(third)
+    o_small[96:104, :] = s3_out[0:8, :]
+    o_small[104:168, :] = t_out[1024:1088, :]
+    net.drain()
+
+
+def unpack(
+    gp, bulk, tail, small,
+    o_points, o_mid, o_feat, o_out, o_up, o_down,
+    o_one, o_two, o_slice, o_temp, o_q, o_k, o_v,
+    sems,
+):
+    stores = [pltpu.make_async_copy(gp, o_points, sems.at[0])]
+    stores[0].start()
 
     def store_columns(src, at, out, count, sem):
         for j in range(count):
             copy = pltpu.make_async_copy(
                 src.at[pl.ds(256 * (at + j), 256), :],
                 out.at[:, pl.ds(128 * j, 128)],
-                out_sems.at[sem + j],
+                sems.at[sem + j],
             )
             copy.start()
             stores.append(copy)
 
-    store_columns(b_out, 0, o_up, 8, 1)
-    store_columns(b_out, 8, o_down, 8, 9)
-    store_columns(b_out, 16, o_out, 2, 17)
-    finish_of(tail)
-    store_columns(t_out, 0, o_mid, 2, 19)
-    store_columns(t_out, 2, o_feat, 2, 21)
-    o_slice[...] = dg(t_out[1024:1056, :], hot4, 1, 0, EXACT)
+    store_columns(bulk, 0, o_up, 8, 1)
+    store_columns(bulk, 8, o_down, 8, 9)
+    store_columns(bulk, 16, o_out, 2, 17)
+    store_columns(tail, 0, o_mid, 2, 19)
+    store_columns(tail, 2, o_feat, 2, 21)
+    hot4 = one_hot_rows(128)
+    for i, o in enumerate((o_q, o_k, o_v)):
+        o[...] = dg(small[32 * i : 32 * (i + 1), :], hot4, 1, 0, EXACT)
+    o_slice[...] = dg(small[104:136, :], hot4, 1, 0, EXACT)
     diag = iota((32, 128), 0) == iota((32, 128), 1)
-    o_temp[...] = jnp.sum(jnp.where(diag, t_out[1056:1088, :], 0.0), axis=0, keepdims=True)[:, 0:32]
-    o_one[:, 0:128] = t_out[1088:1089, :]
-    o_one[:, 128:256] = t_out[1089:1090, :]
-    o_two[:, 0:128] = t_out[1090:1091, :]
-    o_two[:, 128:256] = t_out[1091:1092, :]
+    o_temp[...] = jnp.sum(jnp.where(diag, small[136:168, :], 0.0), axis=0, keepdims=True)[:, 0:32]
+    o_one[:, 0:128] = small[96:97, :]
+    o_one[:, 128:256] = small[97:98, :]
+    o_two[:, 0:128] = small[98:99, :]
+    o_two[:, 128:256] = small[99:100, :]
     for store in stores:
         store.wait()
-    net.drain()
 
 
 def call(active, n, args):
@@ -698,29 +726,31 @@
         + [vm(64, 128), vm(64, 384), vm(64, 128), vm(64, 128), vb(C, C), vb(C, 768), vb(C, 512), vm(C, 128)]
         + [vm(FF, n), vb(C, n), vb(C, n), vm(C, NB), vb(FF, n), vb(FF, n), vm(C, n), vb(C, n), vb(C, n),
            vm(C, 128), vm(C, 128)]
-        + [vb(512, n), vb(16, n), vb(512, n), vb(n, C)]
+        + [vb(512, n), vb(16, n), vb(512, n)]
+        + small
         + small
         + small
         + [vm(ROWS_G, 128), vm(2304, 128), vm(2304, 128), vm(9 * 192, 128), vm(576, 128), vm(9 * 48, 128),
-           vm(12 * 48, 128), vm(ROWS_G, 128)]
-        + [vm(ROWS_T, 128), vm(576, 128), vm(576, 128), vm(9 * 48, 128), vm(12 * 48, 128), vm(12 * 48, 128),
-           vm(ROWS_T, 128)]
-        + [pltpu.SemaphoreType.DMA((7,)), pltpu.SemaphoreType.DMA((23,)),
-           pltpu.SemaphoreType.DMA((160,)), pltpu.SemaphoreType.DMA((160,))]
+           vm(12 * 48, 128)]
+        + [vm(ROWS_T, 128), vm(576, 128), vm(576, 128), vm(9 * 48, 128), vm(12 * 48, 128), vm(12 * 48, 128)]
+        + [pltpu.SemaphoreType.DMA((7,)),
+           pltpu.SemaphoreType.DMA((192,)), pltpu.SemaphoreType.DMA((192,))]
     )
 
     def body(*refs):
         kernel(active, *refs)
 
-    outs = pl.pallas_call(
+    mid_shape = [pltpu.VMEM((n, C), BF), pltpu.VMEM((ROWS_G, 128), F32), pltpu.VMEM((ROWS_T, 128), F32),
+                 pltpu.VMEM((168, 128), F32)]
+    packed = pl.pallas_call(
         body,
         name="block_backward",
-        out_shape=out_shape,
+        out_shape=mid_shape,
         in_specs=[any_spec] * 7 + [vmem_spec] * 7,
-        out_specs=[any_spec] * 6 + [vmem_spec] * 7,
+        out_specs=[vmem_spec] * 4,
         scratch_shapes=scratch,
         compiler_params=pltpu.CompilerParams(
-            vmem_limit_bytes=62 * 2**20,
+            vmem_limit_bytes=56 * 2**20,
             has_side_effects=True,
             **({"collective_id": 0} if active else {}),
         ),
@@ -728,6 +758,15 @@
         points, cotangent, w_mid, w_feat, w_out, w_up, w_down,
         gain_one.reshape(1, C), gain_two.reshape(1, C), w_slice, w_temp.reshape(1, 32), w_q, w_k, w_v,
     )
+    outs = pl.pallas_call(
+        unpack,
+        name="unpack",
+        out_shape=out_shape,
+        in_specs=[vmem_spec] * 4,
+        out_specs=[any_spec] * 6 + [vmem_spec] * 7,
+        scratch_shapes=[pltpu.SemaphoreType.DMA((23,))],
+        compiler_params=pltpu.CompilerParams(vmem_limit_bytes=4 * 2**20),
+    )(*packed)
     outs = list(outs)
     outs[6], outs[7], outs[9] = outs[6].reshape(C), outs[7].reshape(C), outs[9].reshape(32)
     return tuple(outs)

time: 110 us -> 85.1 us (0.77)
  Pallas kernels: 97.6 us -> 84 us
  local copies, waits for them, and re-layouts: 11.4 us -> 0 us
    pallas_call x1 -> x2, Pallas kernels: 97.6 us -> 84 us  [the longest x1 81.3 us: call(): pl.pallas_call(body, name='block_backward', out_shape=mid_shape, in_specs...]
    unnamed x37 -> x0, local copies, waits for them, and re-layouts: 11.4 us -> none
where the time goes in v2:
time: 85.1 us; the launch traced here: 84.9 us
  Pallas kernels  84 us (99%)
    pallas_call x1, Pallas kernels, call(): pl.pallas_call(body, name='block_backward', out_shape=mid_shape, in_specs...  81.3 us
    pallas_call x1, Pallas kernels, call(): pl.pallas_call(unpack, name='unpack', out_shape=out_shape, in_specs=[vmem...  2.75 us

profile of v2, /device:TPU:1, one launch (start us, length us, event | category | flops | bytes accessed | tf_op | source)
XLA Modules:
  0.0 84.9 jit_solution(8236246060691283050)
XLA Ops:
  0.7 81.3 %block_backward.1 = (bf16[2048,256]{1,0:T(8,128)(2,1)S(1)}, f32[4608,128]{1,0:T(8,128)S(1)}, f32[1152,128]{1,0:T(8,128)S(1)}, f32[168,128]{1,0:T(8,128)S(1)}) custom-call(bf16[2048,256]{1,0:T(8,128)(2,1)} %refs_0_.1, bf16[2048,256]{1,0:T(8,128)(2,1)} %refs_1_.1, bf16[256,256]{1,0:T(8,128)(2,1)} %refs_2_.1, bf16[256,256]{1,0:T(8,128)(2,1)} %refs_3_.1, ...), custom_call_target="tpu_custom_call" | custom-call | tf_op jit(solution)/shard_map/block_backward/pallas_call | solution.py:745
  82.0 2.7 %unpack.1 = (bf16[2048,256]{1,0:T(8,128)(2,1)}, f32[256,256]{1,0:T(8,128)}, f32[256,256]{1,0:T(8,128)}, f32[256,256]{1,0:T(8,128)}, f32[256,1024]{1,0:T(8,128)},...) custom-call(bf16[2048,256]{1,0:T(8,128)(2,1)S(1)} %get-tuple-element, ...), custom_call_target="tpu_custom_call" | custom-call | tf_op jit(solution)/shard_map/unpack/pallas_call | solution.py:761

commit v3 on v2

--- a/solution.py
+++ b/solution.py
@@ -96,29 +96,42 @@
             self.core = core
             self.at = (x, y, z)
             self.partner = (pts + 1 - 2 * core, z)
+            other = 1 - core
             self.peer = (
                 lambda j: (j * 8 + y * 2 + core, z),
                 lambda j: (x * 8 + j * 2 + core, z),
                 lambda j: (pts, j),
             )
+            self.cross = (
+                lambda j: (j * 8 + y * 2 + other, z),
+                lambda j: (x * 8 + j * 2 + other, z),
+                lambda j: (x * 8 + y * 2 + other, j),
+            )
+
+    def eight(self, ax):
+        out = []
+        for d in range(4):
+            j = (self.at[ax] + d) % 4
+            if d > 0:
+                out.append((2 * d, j, self.core, self.peer[ax](j)))
+            out.append((2 * d + 1, j, 1 - self.core, self.cross[ax](j)))
+        return out
 
     def hello(self):
         if not self.active:
             return
         barrier = pltpu.get_barrier_semaphore()
-        pl.semaphore_signal(barrier, inc=1, device_id=self.partner, device_id_type=MESH)
+        devices = [self.partner]
         for ax in range(3):
             for d in range(1, 4):
-                pl.semaphore_signal(
-                    barrier,
-                    inc=1,
-                    device_id=self.peer[ax]((self.at[ax] + d) % 4),
-                    device_id_type=MESH,
-                )
+                j = (self.at[ax] + d) % 4
+                devices += [self.peer[ax](j), self.cross[ax](j)]
+        for device in devices:
+            pl.semaphore_signal(barrier, inc=1, device_id=device, device_id_type=MESH)
 
     def ready(self):
         if self.active:
-            pl.semaphore_wait(pltpu.get_barrier_semaphore(), 10)
+            pl.semaphore_wait(pltpu.get_barrier_semaphore(), 19)
 
     def send(self, src, dst, device):
         k = self.count
@@ -145,36 +158,39 @@
     return pl.ds(pl.multiple_of(start, 8), size)
 
 
-def small_sum(net, src, from_core, slots, out):
+def add_all(v):
+    while len(v) > 1:
+        v = [v[k] + v[k + 1] for k in range(0, len(v), 2)]
+    return v[0]
+
+
+def small_sum(net, src, slots, out):
     if not net.active:
         out[...] = src[...]
         return
-    copy = net.send(src, from_core, net.partner)
-    yield
-    copy.wait_recv()
-    parts = [
-        src[PART_S * p : PART_S * (p + 1), :] + from_core[PART_S * p : PART_S * (p + 1), :]
-        for p in range(3)
-    ]
+    parts = [src[PART_S * p : PART_S * (p + 1), :] for p in range(3)]
+    base = 0
     for k in range(3):
+        wide = 8 if k == 0 else 4
         copies = []
         for p in range(3):
             ax = (p + k) % 3
-            mine = rows(k * 12 * PART_S + (p * 4 + net.at[ax]) * PART_S, PART_S)
+            here = 2 * net.at[ax] + net.core if k == 0 else net.at[ax]
+            mine = rows(base + (p * wide + here) * PART_S, PART_S)
             slots[mine, :] = parts[p]
-            for d in range(1, 4):
-                copies.append(
-                    net.send(slots.at[mine, :], slots.at[mine, :], net.peer[ax]((net.at[ax] + d) % 4))
-                )
+            devices = [item[3] for item in net.eight(ax)]
+            if k > 0:
+                devices = [net.peer[ax]((net.at[ax] + d) % 4) for d in range(1, 4)]
+            for device in devices:
+                copies.append(net.send(slots.at[mine, :], slots.at[mine, :], device))
         yield
         for copy in copies:
             copy.wait_recv()
         for p in range(3):
-            four = [
-                slots[pl.ds(k * 12 * PART_S + (p * 4 + s) * PART_S, PART_S), :]
-                for s in range(4)
-            ]
-            parts[p] = (four[0] + four[1]) + (four[2] + four[3])
+            parts[p] = add_all(
+                [slots[pl.ds(base + (p * wide + t) * PART_S, PART_S), :] for t in range(wide)]
+            )
+        base += 3 * wide * PART_S
     for p in range(3):
         out[PART_S * p : PART_S * (p + 1), :] = parts[p]
 
@@ -286,34 +302,44 @@
     yield from core_gather(net, out, lambda p: rows(base(p, 0), half))
 
 
-def tail_sum(net, src, got0, sum0, got1, slots1, slots2, out):
+def tail_sum(net, src, got, slots1, slots2, out):
     if not net.active:
         out[...] = src[...]
         return
-    part, half, piece = 384, 192, 48
-    yield from core_scatter(net, src, got0, sum0, part)
-
-    def keep(slots, k):
-        def store(p, v):
-            slots[rows((p * 4 + net.at[(p + k) % 3]) * piece, piece), :] = v
-
-        return store
-
-    yield from axis_scatter(net, 0, sum0, got1, half, keep(slots1, 1))
-    yield from axis_exchange(net, 1, slots1, piece, keep(slots2, 2))
-
-    def where(p, depth):
-        at = p * part + net.core * half
-        if depth > 0:
-            at = at + net.at[p % 3] * piece
-        return rows(at, piece if depth else half)
+    part, piece = 384, 48
+
+    def where(p, j, core):
+        return rows(p * part + (2 * j + core) * piece, piece)
+
+    copies = []
+    for p in range(3):
+        for t, j, core, device in net.eight(p):
+            there = got.at[pl.ds((p * 8 + t) * piece, piece), :]
+            copies.append(net.send(src.at[where(p, j, core), :], there, device))
+    yield
+    for copy in copies:
+        copy.wait_recv()
+    for p in range(3):
+        terms = [src[where(p, net.at[p], net.core), :]]
+        terms += [got[pl.ds((p * 8 + t) * piece, piece), :] for t in range(1, 8)]
+        slots1[rows((p * 4 + net.at[(p + 1) % 3]) * piece, piece), :] = add_all(terms)
+
+    def keep(p, v):
+        slots2[rows((p * 4 + net.at[(p + 2) % 3]) * piece, piece), :] = v
+
+    yield from axis_exchange(net, 1, slots1, piece, keep)
 
     def last(p, v):
-        out[where(p, 1), :] = v
+        out[where(p, net.at[p], net.core), :] = v
 
     yield from axis_exchange(net, 2, slots2, piece, last)
-    yield from axis_gather(net, 0, out, lambda p: where(p, 1))
-    yield from core_gather(net, out, lambda p: where(p, 0))
+    copies = []
+    for p in range(3):
+        here = out.at[where(p, net.at[p], net.core), :]
+        copies += [net.send(here, here, item[3]) for item in net.eight(p)]
+    yield
+    for copy in copies:
+        copy.wait_recv()
 
 
 def step_of(gen):
@@ -337,10 +363,10 @@
     tok_s, qkv_s, prob_s, denb_s, mixT, lhs_c, dnT, ddc,
     dhT, sT, n2T, xh2, hT, dpT, drT, drb, dsT, ga1, ga2,
     dl_s, dt_s, dmf_s,
-    s1_src, s1_core, s1_slots, s1_out, s2_src, s2_core, s2_slots, s2_out,
-    s3_src, s3_core, s3_slots, s3_out,
+    s1_src, s1_slots, s1_out, s2_src, s2_slots, s2_out,
+    s3_src, s3_slots, s3_out,
     b_src, b_got0, b_sum0, b_got1, b_sum1, b_got2, b_slots,
-    t_src, t_got0, t_sum0, t_got1, t_slots1, t_slots2,
+    t_src, t_got, t_slots1, t_slots2,
     in_sems, send_sems, recv_sems,
 ):
     n = pts_v.shape[0]
@@ -424,7 +450,7 @@
     s1_src[64:72, :] = jnp.concatenate(den_rows + [jnp.zeros((6, 128), F32)], axis=0)
 
     net.ready()
-    first = small_sum(net, s1_src, s1_core, s1_slots, s1_out)
+    first = small_sum(net, s1_src, s1_slots, s1_out)
     step_of(first)
 
     slice_n = jnp.where(mask, dg(dg(hot, w_slice[...], 1, 0, EXACT), hot, 1, 1, EXACT), 0.0)
@@ -521,7 +547,7 @@
         rear(i, 0)
     s2_src[0:64, :] = fold_diagonal(dg(wb[...], dsT[...], 1, 1))
     s2_src[64:72, :] = jnp.zeros((8, 128), F32)
-    second = small_sum(net, s2_src, s2_core, s2_slots, s2_out)
+    second = small_sum(net, s2_src, s2_slots, s2_out)
     step_of(second)
 
     def put(left, right, at):
@@ -534,13 +560,12 @@
         fr = slice(256 * f, 256 * f + 256)
         put(n2T[...], dpT[fr, :], 2 * f)
         put(cT[...], hT[fr, :], 8 + 2 * f)
-        if f == 1:
-            step_of(second)
     put(sT[...], drb[...], 16)
     step_of(bulk)
     step_of(second)
     step_of(bulk)
     step_of(second)
+    step_of(bulk)
     finish_of(second)
 
     dqs, dks, dvs = [], [], []
@@ -619,8 +644,8 @@
 
     for i in range(chunks):
         finish(i)
-        step_of(bulk)
-
+
+    step_of(bulk)
     gmf = dg(nT[...], dmf_s[...], 1, 1)
     for j in range(4):
         t_src[256 * j : 256 * (j + 1), :] = gmf[:, 128 * j : 128 * (j + 1)]
@@ -635,30 +660,28 @@
     for h in range(1, HEADS):
         gt32 = gt32 + gt[32 * h : 32 * h + 32]
     t_src[1056:1088, :] = jnp.broadcast_to(gt32, (32, 128))
-    tail = tail_sum(net, t_src, t_got0, t_sum0, t_got1, t_slots1, t_slots2, t_out)
+    tail = tail_sum(net, t_src, t_got, t_slots1, t_slots2, t_out)
     step_of(tail)
-    points_gradient(0)
-    step_of(tail)
-    for i in range(1, chunks):
+    for i in range(chunks):
         points_gradient(i)
     gain_rows = column_to_rows(jnp.sum(ga1[...], axis=1, keepdims=True)) + column_to_rows(
         jnp.sum(ga2[...], axis=1, keepdims=True)
     )
     s3_src[0:8, :] = jnp.concatenate(gain_rows + [jnp.zeros((4, 128), F32)], axis=0)
     s3_src[8:ROWS_S, :] = jnp.zeros((ROWS_S - 8, 128), F32)
-    third = small_sum(net, s3_src, s3_core, s3_slots, s3_out)
+    third = small_sum(net, s3_src, s3_slots, s3_out)
     step_of(third)
     step_of(bulk)
-    step_of(third)
+    step_of(tail)
 
     for i, d in enumerate((dqs, dks, dvs)):
         full = jnp.where(mask4, dg(tok, jnp.concatenate(d, axis=0), 0, 0, EXACT), 0.0)
         o_small[32 * i : 32 * (i + 1), :] = dg(hot4, full, 0, 0, EXACT)
 
     for _ in range(8):
+        step_of(third)
+        step_of(bulk)
         step_of(tail)
-        step_of(bulk)
-        step_of(third)
     o_small[96:104, :] = s3_out[0:8, :]
     o_small[104:168, :] = t_out[1024:1088, :]
     net.drain()
@@ -717,7 +740,7 @@
         + [jax.ShapeDtypeStruct((32, 32), F32), jax.ShapeDtypeStruct((1, 32), F32)]
         + [jax.ShapeDtypeStruct((32, 32), F32)] * 3
     )
-    small = [vm(ROWS_S, 128), vm(ROWS_S, 128), vm(36 * PART_S, 128), vm(ROWS_S, 128)]
+    small = [vm(ROWS_S, 128), vm(48 * PART_S, 128), vm(ROWS_S, 128)]
     scratch = (
         [vb(n, C), vb(n, C), vb(C, C), vb(C, C), vb(C, C), vb(C, FF), vb(C, FF)]
         + [vb(C, n), vb(C, n), vb(512, C), vb(C, 512), vb(C, C), vb(FF, C), vb(FF, C)]
@@ -732,9 +755,9 @@
         + small
         + [vm(ROWS_G, 128), vm(2304, 128), vm(2304, 128), vm(9 * 192, 128), vm(576, 128), vm(9 * 48, 128),
            vm(12 * 48, 128)]
-        + [vm(ROWS_T, 128), vm(576, 128), vm(576, 128), vm(9 * 48, 128), vm(12 * 48, 128), vm(12 * 48, 128)]
+        + [vm(ROWS_T, 128), vm(24 * 48, 128), vm(12 * 48, 128), vm(12 * 48, 128)]
         + [pltpu.SemaphoreType.DMA((7,)),
-           pltpu.SemaphoreType.DMA((192,)), pltpu.SemaphoreType.DMA((192,))]
+           pltpu.SemaphoreType.DMA((256,)), pltpu.SemaphoreType.DMA((256,))]
     )
 
     def body(*refs):

time: 85.1 us -> 78.6 us (0.924)
  Pallas kernels: 84 us -> 77.6 us
    pallas_call x1, Pallas kernels: 81.3 us -> 74.9 us  [call(): pl.pallas_call(body, name='block_backward', out_shape=mid_shape, in_specs...]
where the time goes in v3:
time: 78.6 us; the launch traced here: 78.4 us
  Pallas kernels  77.6 us (99%)
  between operations  0.84 us (1%)
    pallas_call x1, Pallas kernels, call(): pl.pallas_call(body, name='block_backward', out_shape=mid_shape, in_specs...  74.9 us
    pallas_call x1, Pallas kernels, call(): pl.pallas_call(unpack, name='unpack', out_shape=out_shape, in_specs=[vmem...  2.75 us

profile of v3, /device:TPU:1, one launch (start us, length us, event | category | flops | bytes accessed | tf_op | source)
XLA Modules:
  0.0 78.4 jit_solution(2718901173125006840)
XLA Ops:
  0.7 74.9 %block_backward.1 = (bf16[2048,256]{1,0:T(8,128)(2,1)S(1)}, f32[4608,128]{1,0:T(8,128)S(1)}, f32[1152,128]{1,0:T(8,128)S(1)}, f32[168,128]{1,0:T(8,128)S(1)}) custom-call(bf16[2048,256]{1,0:T(8,128)(2,1)} %refs_0_.1, bf16[2048,256]{1,0:T(8,128)(2,1)} %refs_1_.1, bf16[256,256]{1,0:T(8,128)(2,1)} %refs_2_.1, bf16[256,256]{1,0:T(8,128)(2,1)} %refs_3_.1, ...), custom_call_target="tpu_custom_call" | custom-call | tf_op jit(solution)/shard_map/block_backward/pallas_call | solution.py:768
  75.5 2.7 %unpack.1 = (bf16[2048,256]{1,0:T(8,128)(2,1)}, f32[256,256]{1,0:T(8,128)}, f32[256,256]{1,0:T(8,128)}, f32[256,256]{1,0:T(8,128)}, f32[256,1024]{1,0:T(8,128)},...) custom-call(bf16[2048,256]{1,0:T(8,128)(2,1)S(1)} %get-tuple-element, ...), custom_call_target="tpu_custom_call" | custom-call | tf_op jit(solution)/shard_map/unpack/pallas_call | solution.py:784
